TPU v7x, 32 devices: a whole 2x2x4 slice. The times are simulated.
32 devices in a mesh: blk: 8 (over y, x, core), lines: 4 (over z).
Axes of the slice: x: 2, y: 2, z: 4, core: 2. Of those that a mesh axis runs over, the one named last changes fastest.
Arguments:
- velocity: float32 [3, 12288, 1024], P(None, 'lines', 'blk'), may hold values from -6 to 6
- metric: float32 [1024], P('blk'), may hold values from 0.5 to 2
Outputs:
- derivs: float32 [3, 12288, 1024], P(None, 'lines', 'blk')
- profile: float32 [1024], P('blk')
All inputs are finite; a program needn't handle non-finite values.
Results may differ from a plain program's by a relative error of at most 0.00007.
Values sent between devices are 32-bit elements; how exact they have to be, the bound alone decides.
No kernel may reach another device: no remote copies, remote signals or barrier semaphores. Data moves between devices by JAX's collectives and lax.ppermute only.
A program may use at most 128 MiB of HBM per device.

v0:
```python
import jax
import jax.numpy as jnp
from jax import lax
from jax.sharding import PartitionSpec as P

ALPHA = 1.0 / 3.0
COEF_A = 7.0 / 9.0
COEF_B = 1.0 / 36.0


def block_inverse(width):
    counter = jnp.arange(width, dtype=jnp.int32) + 1
    product = counter[:, None] * counter[None, :] % (2 * (width + 1))
    angles = jnp.pi / (width + 1.0)
    sines = jnp.sqrt(2.0 / (width + 1.0)) * jnp.sin(angles * product.astype(jnp.float32))
    eigen = 1.0 + 2.0 * ALPHA * jnp.cos(angles * counter.astype(jnp.float32))
    return jnp.dot(sines / eigen[None, :], sines, precision=lax.Precision.HIGHEST)


def solve_rows(source, inverse):
    shape = source.shape
    flat = jnp.dot(source.reshape(-1, shape[-1]), inverse, precision=lax.Precision.HIGHEST)
    return flat.reshape(shape)


def interface(first_own, last_own, last_left, first_right, couple):
    factor = 1.0 / (1.0 - couple * couple)
    last_prev = (last_left - couple * first_own) * factor
    last_here = (last_own - couple * first_right) * factor
    first_next = first_right - couple * last_here
    return (last_prev, first_next)


def correct(partial_value, inverse, last_prev, first_next):
    width = inverse.shape[0]
    return partial_value - ALPHA * (
        last_prev[..., None] * inverse[:, 0] + first_next[..., None] * inverse[:, width - 1]
    )


def local(velocity, metric):
    width = velocity.shape[2]
    inverse = block_inverse(width)
    couple = ALPHA * inverse[0, 0]
    lines_block = lax.all_to_all(velocity, "blk", split_axis=1, concat_axis=2, tiled=True)
    count = lines_block.shape[-1]
    source = COEF_A * (jnp.roll(lines_block, -1, -1) - jnp.roll(lines_block, 1, -1)) + COEF_B * (
        jnp.roll(lines_block, -2, -1) - jnp.roll(lines_block, 2, -1)
    )
    blocks = source.reshape(lines_block.shape[0], lines_block.shape[1], count // width, width)
    partial_value = solve_rows(blocks, inverse)
    first_own = partial_value[..., 0]
    last_own = partial_value[..., width - 1]
    last_prev, first_next = interface(
        first_own, last_own, jnp.roll(last_own, 1, 2), jnp.roll(first_own, -1, 2), couple
    )
    whole = correct(partial_value, inverse, last_prev, first_next).reshape(lines_block.shape)
    solved = lax.all_to_all(whole, "blk", split_axis=2, concat_axis=1, tiled=True)
    derivs = solved * metric
    squares = jnp.sum(derivs * derivs, axis=(0, 1))
    total = lax.psum(squares, "lines")
    profile = total / (velocity.shape[1] * lax.axis_size("lines"))
    return (derivs, profile)


def solution(mesh):
    in_specs = (P(None, "lines", "blk"), P("blk"))
    out_specs = (P(None, "lines", "blk"), P("blk"))
    return jax.shard_map(local, mesh=mesh, in_specs=in_specs, out_specs=out_specs, check_vma=False)
```

profile of v0, /device:TPU:0, one launch (start us, length us, event | category | flops | bytes accessed | tf_op | source)
XLA Modules:
  0.0 224.0 jit_solution(313442755634897913)
XLA Ops:
  0.6 8.7 %copy.19 = f32[3,3072,128]{2,0,1:T(4,128)} copy(f32[3,3072,128]{2,1,0:T(8,128)} %param.2) | data formatting | bytes 9437184 | tf_op args[0]
  9.3 5.2 %all-to-all-start = ((f32[3,3072,128]{2,0,1:T(4,128)}), f32[3,3072,128]{2,0,1:T(4,128)}, u32[]{:S(2)}, u32[]{:S(2)}) async-start(f32[3,3072,128]{2,0,1:T(4,128)} %copy.19), calls=%async_computation | async-start | bytes 12582912 | tf_op jit(solution)/shard_map/all_to_all | solution.py:45
  14.6 0.9 fusion.3
  15.4 0.5 slice.91
  17.9 68.4 %all-to-all-done = f32[3,3072,128]{2,0,1:T(4,128)} async-done(((f32[3,3072,128]{2,0,1:T(4,128)}), f32[3,3072,128]{2,0,1:T(4,128)}, u32[]{:S(2)}, u32[]{:S(2)}) %all-to-all-start) | async-done | bytes 4718624 | tf_op jit(solution)/shard_map/all_to_all | solution.py:45
  86.3 5.3 %copy.20 = f32[3,3072,128]{2,1,0:T(8,128)} copy(f32[3,3072,128]{2,0,1:T(4,128)} %all-to-all-done) | data formatting | bytes 9437184 | tf_op jit(solution)/shard_map/all_to_all | solution.py:45
  91.6 6.1 %copy.21 = f32[3,384,8,128]{1,3,2,0:T(8,128)} copy(f32[3,384,8,128]{3,1,2,0:T(8,128)} %bitcast.50) | data formatting | bytes 9437184 | tf_op jit(solution)/shard_map/all_to_all | solution.py:45
  97.7 0.0 copy-start
  97.7 4.5 %fusion.33 = (f32[3,384,1023]{1,2,0:T(8,128)S(1)}, f32[3,384,1023]{1,2,0:T(8,128)S(1)}) fusion(f32[3,384,1024]{1,2,0:T(8,128)} %bitcast.42), kind=kLoop, calls=%fused_computation.53 | loop fusion | bytes 18855936 | tf_op jit(solution)/shard_map/jit(_roll_static)/slice | solution.py:47
  102.2 0.6 copy-done
  102.8 2.8 %fusion.31 = (f32[3,384,1022]{1,2,0:T(8,128)S(1)}, f32[3,384,1022]{1,2,0:T(8,128)}) fusion(f32[3,384,1024]{1,2,0:T(8,128)S(1)} %bitcast.43), kind=kLoop, calls=%fused_computation.51 | loop fusion | bytes 18837504 | tf_op jit(solution)/shard_map/jit(_roll_static)/slice | solution.py:48
  105.6 6.7 %fusion.1 = f32[3,384,1024]{1,2,0:T(8,128)S(1)} fusion(f32[3,384,1]{1,2,0:T(1,128)S(1)} %get-tuple-element.9, f32[3,384,1023]{1,2,0:T(8,128)S(1)} %get-tuple-element.11, f32[3,384,1023]{1,2,0:T(8,128)S(1)} %get-tuple-element.10, f32[3,384,1]{1,2,0:T(1,128)S(1)} %get-tuple-element.8, f32[3,384,2]{1,2,0:T(2,128)S(1)} %get-tuple-element.5, ...), kind=kLoop, calls=%fused_computation.3 | loop fusion | flops 10616832 | bytes 23592960 | tf_op jit(solution)/shard_map/add | solution.py:47
  112.3 4.7 %fusion.10 = f32[3,384,8,128]{1,3,2,0:T(8,128)S(1)} fusion(f32[3,384,8,128]{1,3,2,0:T(8,128)S(1)} %bitcast.48, f32[128,128]{0,1:T(8,128)S(1)} %fusion.3), kind=kOutput, calls=%fused_computation.15 | convolution fusion | flops 1811939328 | bytes 9502720 | tf_op jit(solution)/shard_map/dot_general | solution.py:22
  117.1 0.1 fusion.29
  117.3 1.0 multiply_subtract_fusion
  118.3 3.2 %copy.26 = f32[3,384,1024]{1,0,2:T(4,128)S(1)} copy(f32[3,384,1024]{1,2,0:T(8,128)S(1)} %bitcast.49) | data formatting | bytes 9437184 | tf_op jit(solution)/shard_map/reshape | solution.py:57
  121.5 74.9 %all_to_all.36 = f32[3,384,1024]{1,0,2:T(4,128)} all-to-all(f32[3,384,1024]{1,0,2:T(4,128)S(1)} %copy.26), channel_id=1, replica_groups=mesh['blk'=8,'lines'=4] {'blk'}, dimensions={2} | all-to-all | bytes 9437184 | tf_op jit(solution)/shard_map/all_to_all | solution.py:58
  196.4 0.0 copy-start.2
  196.4 6.9 %copy.27 = f32[3,8,384,128]{3,2,1,0:T(8,128)} copy(f32[3,8,384,128]{2,0,3,1:T(4,128)} %bitcast.46) | data formatting | bytes 9437184 | tf_op jit(solution)/shard_map/all_to_all | solution.py:58
  203.3 0.0 copy-done.2
  203.3 0.0 copy-start.1
  203.3 4.9 %multiply_reduce_fusion = f32[128]{0:T(128)S(1)} fusion(f32[3,8,384,128]{2,0,3,1:T(4,128)} %bitcast.47, f32[128]{0:T(128)S(1)} %copy-done.2), kind=kLoop, calls=%fused_computation | loop fusion | flops 3538816 | bytes 4719616 | tf_op jit(solution)/shard_map/reduce_sum | solution.py:60
  208.3 0.0 copy-done.1
  208.3 2.5 %bitcast_multiply_fusion = f32[3,3072,128]{2,1,0:T(8,128)} fusion(f32[3,8,384,128]{3,2,1,0:T(8,128)S(1)} %copy-done.1, f32[128]{0:T(128)S(1)} %copy-done.2), kind=kLoop, calls=%fused_computation.6 | loop fusion | flops 1179648 | bytes 9437696 | tf_op jit(solution)/shard_map/mul | solution.py:59
  210.8 12.7 %psum.7 = f32[128]{0:T(128)S(1)} all-reduce(f32[128]{0:T(128)S(1)} %multiply_reduce_fusion), channel_id=1, replica_groups=mesh['blk'=8,'lines'=4] {'lines'}, use_global_device_ids=true, to_apply=%region_1.2 | all-reduce | flops 128 | bytes 1024 | tf_op jit(solution)/shard_map/psum | solution.py:61
  223.5 0.5 broadcast_multiply_fusion
  (12 shorter events, 0.1 us)
Async XLA Ops:
  9.3 77.0 %all-to-all-start = ((f32[3,3072,128]{2,0,1:T(4,128)}), f32[3,3072,128]{2,0,1:T(4,128)}, u32[]{:S(2)}, u32[]{:S(2)}) async-start(f32[3,3072,128]{2,0,1:T(4,128)} %copy.19), calls=%async_computation | async-start | bytes 12582912 | tf_op jit(solution)/shard_map/all_to_all | solution.py:45
  97.7 5.1 %copy-start = (f32[3,384,8,128]{1,3,2,0:T(8,128)S(1)}, f32[3,384,8,128]{1,3,2,0:T(8,128)}, u32[]{:S(2)}) copy-start(f32[3,384,8,128]{1,3,2,0:T(8,128)} %copy.21) | copy-start | bytes 14155780
  196.4 6.9 %copy-start.2 = (f32[128]{0:T(128)S(1)}, f32[128]{0:T(128)}, u32[]{:S(2)}) copy-start(f32[128]{0:T(128)} %param.3) | copy-start | bytes 1540
  203.3 5.0 %copy-start.1 = (f32[3,8,384,128]{3,2,1,0:T(8,128)S(1)}, f32[3,8,384,128]{3,2,1,0:T(8,128)}, u32[]{:S(2)}) copy-start(f32[3,8,384,128]{3,2,1,0:T(8,128)} %copy.27) | copy-start | bytes 14155780
where the time goes:
time: 225 us; the launch traced here: 224 us
  blocking collectives  87.6 us (39%)
  waiting for transfers between devices  68.4 us (30%)
  local copies, waits for them, and re-layouts  38.7 us (17%)
  other arithmetic  15.8 us (7%)
  matrix products  5.58 us (2%)
  starting transfers between devices  5.17 us (2%)
  between operations  2.74 us (1%)
    all_to_all x1, blocking collectives, local(): lax.all_to_all(whole, 'blk', split_axis=2, concat_axis=1, tiled=True)  74.9 us
    all_to_all x1, waiting for transfers between devices, local(): lax.all_to_all(velocity, 'blk', split_axis=1, concat_axis=2, tiled=True)  68.4 us
    psum x1, blocking collectives, local(): total = lax.psum(squares, 'lines')  12.7 us
    all_to_all x2, local copies, waits for them, and re-layouts, local(): lax.all_to_all(velocity, 'blk', split_axis=1, concat_axis=2, tiled=True)  11.3 us
    unnamed x8, local copies, waits for them, and re-layouts  9.3 us
    all_to_all x1, local copies, waits for them, and re-layouts, local(): lax.all_to_all(whole, 'blk', split_axis=2, concat_axis=1, tiled=True)  6.91 us
    add x1, other arithmetic, local(): COEF_A * (jnp.roll(lines_block, -1, -1) - jnp.roll(lines_block, 1, -1))  6.72 us
    all_to_all x1, starting transfers between devices, local(): lax.all_to_all(velocity, 'blk', split_axis=1, concat_axis=2, tiled=True)  5.17 us
  transfers between devices with their start and end apart: 1, of which 1 were waited for; matrix products, arithmetic and copies ran while one was open for 1% of the time, Pallas kernels for 0%

commit v1 on v0

--- a/solution.py
+++ b/solution.py
@@ -6,6 +6,13 @@
 ALPHA = 1.0 / 3.0
 COEF_A = 7.0 / 9.0
 COEF_B = 1.0 / 36.0
+
+
+def swap_blocks(x, axis, split, join):
+    peers = lax.axis_size(axis)
+    blocks = jnp.stack(jnp.split(x, peers, axis=split), axis=0)
+    blocks = lax.all_to_all(blocks, axis, split_axis=0, concat_axis=0)
+    return jnp.concatenate(blocks, axis=join)
 
 
 def block_inverse(width):
@@ -42,7 +49,7 @@
     width = velocity.shape[2]
     inverse = block_inverse(width)
     couple = ALPHA * inverse[0, 0]
-    lines_block = lax.all_to_all(velocity, "blk", split_axis=1, concat_axis=2, tiled=True)
+    lines_block = swap_blocks(velocity, "blk", 1, 2)
     count = lines_block.shape[-1]
     source = COEF_A * (jnp.roll(lines_block, -1, -1) - jnp.roll(lines_block, 1, -1)) + COEF_B * (
         jnp.roll(lines_block, -2, -1) - jnp.roll(lines_block, 2, -1)

time: 225 us -> 206 us (0.916)
  waiting for transfers between devices: 68.4 us -> 51.4 us
    all_to_all x1, waiting for transfers between devices: 68.4 us -> 51.4 us  [swap_blocks(): blocks = lax.all_to_all(blocks, axis, split_axis=0, concat_axis=0)]
    all_to_all x2 -> x1, local copies, waits for them, and re-layouts: 11.3 us -> 2.64 us  [swap_blocks(): blocks = lax.all_to_all(blocks, axis, split_axis=0, concat_axis=0)]
    unnamed x8 -> x20, local copies, waits for them, and re-layouts: 9.3 us -> 15.7 us
    slice x2, local copies, waits for them, and re-layouts: 4.52 us -> 0.63 us  [local(): jnp.roll(lines_block, 1, -1)]
    split x0 -> x1, local copies, waits for them, and re-layouts: none -> 3.66 us  [swap_blocks(): blocks = jnp.stack(jnp.split(x, peers, axis=split), axis=0)]
where the time goes in v1:
time: 206 us; the launch traced here: 205 us
  blocking collectives  87.6 us (43%)
  waiting for transfers between devices  51.4 us (25%)
  local copies, waits for them, and re-layouts  37 us (18%)
  other arithmetic  15.8 us (8%)
  matrix products  5.58 us (3%)
  starting transfers between devices  5.17 us (3%)
  between operations  2.76 us (1%)
    all_to_all x1, blocking collectives, local(): lax.all_to_all(whole, 'blk', split_axis=2, concat_axis=1, tiled=True)  74.9 us
    all_to_all x1, waiting for transfers between devices, swap_blocks(): blocks = lax.all_to_all(blocks, axis, split_axis=0, concat_axis=0)  51.4 us
    unnamed x20, local copies, waits for them, and re-layouts  15.7 us
    psum x1, blocking collectives, local(): total = lax.psum(squares, 'lines')  12.7 us
    all_to_all x1, local copies, waits for them, and re-layouts, local(): lax.all_to_all(whole, 'blk', split_axis=2, concat_axis=1, tiled=True)  6.91 us
    add x1, other arithmetic, local(): COEF_A * (jnp.roll(lines_block, -1, -1) - jnp.roll(lines_block, 1, -1))  6.72 us
    all_to_all x1, starting transfers between devices, swap_blocks(): blocks = lax.all_to_all(blocks, axis, split_axis=0, concat_axis=0)  5.17 us
    reduce_sum x1, other arithmetic, local(): squares = jnp.sum(derivs * derivs, axis=(0, 1))  4.95 us
  transfers between devices with their start and end apart: 1, of which 1 were waited for; matrix products, arithmetic and copies ran while one was open for 1% of the time, Pallas kernels for 0%

profile of v1, /device:TPU:0, one launch (start us, length us, event | category | flops | bytes accessed | tf_op | source)
XLA Modules:
  0.0 205.4 jit_solution(2516222494657116879)
XLA Ops:
  0.6 3.7 %fusion.34 = (f32[3,384,128]{2,1,0:T(8,128)S(1)}, f32[3,384,128]{2,1,0:T(8,128)S(1)}, f32[3,384,128]{2,1,0:T(8,128)S(1)}, f32[3,384,128]{2,1,0:T(8,128)S(1)}, f3...) fusion(f32[3,3072,128]{2,1,0:T(8,128)} %param.2), kind=kLoop, calls=%fused_computation.62 | loop fusion | bytes 9437184 | tf_op jit(solution)/shard_map/split | solution.py:13
  4.3 2.1 %copy.39 = f32[3,384,128]{1,2,0:T(8,128)} copy(f32[3,384,128]{2,1,0:T(8,128)} %get-tuple-element.19) | data formatting | bytes 1179648
  6.4 1.9 bitcast_dynamic-update-slice_fusion.7
  8.3 2.1 %copy.40 = f32[3,384,128]{1,2,0:T(8,128)} copy(f32[3,384,128]{2,1,0:T(8,128)} %get-tuple-element.18) | data formatting | bytes 1179648
  10.5 1.1 copy.41
  11.5 0.2 copy.42
  11.8 0.2 copy.43
  12.0 0.2 copy.44
  12.2 0.2 copy.45
  12.5 0.2 copy.46
  12.7 1.9 bitcast_dynamic-update-slice_fusion.6
  14.6 1.9 bitcast_dynamic-update-slice_fusion.5
  16.5 0.9 bitcast_dynamic-update-slice_fusion.4
  17.4 0.9 bitcast_dynamic-update-slice_fusion.3
  18.2 0.9 bitcast_dynamic-update-slice_fusion.2
  19.1 0.9 bitcast_dynamic-update-slice_fusion.1
  20.0 0.9 bitcast_dynamic-update-slice_fusion
  20.8 5.2 %all-to-all-start = ((f32[8,3,384,128]{2,3,1,0:T(8,128)}), f32[8,3,384,128]{2,3,1,0:T(8,128)}, u32[]{:S(2)}, u32[]{:S(2)}) async-start(f32[8,3,384,128]{2,3,1,0:T(8,128)} %bitcast_dynamic-update-slice_fusion), calls=%async_computation | async-start | bytes 9437184 | tf_op jit(solution)/shard_map/all_to_all | solution.py:14
  26.0 0.9 fusion.3
  26.9 0.5 slice.91
  29.4 51.4 %all-to-all-done = f32[8,3,384,128]{2,3,1,0:T(8,128)} async-done(((f32[8,3,384,128]{2,3,1,0:T(8,128)}), f32[8,3,384,128]{2,3,1,0:T(8,128)}, u32[]{:S(2)}, u32[]{:S(2)}) %all-to-all-start) | async-done | bytes 4718624 | tf_op jit(solution)/shard_map/all_to_all | solution.py:14
  80.8 2.6 %copy.29 = f32[8,3,384,128]{2,3,0,1:T(8,128)S(1)} copy(f32[8,3,384,128]{2,3,1,0:T(8,128)} %all-to-all-done) | data formatting | bytes 9437184 | tf_op jit(solution)/shard_map/all_to_all | solution.py:14
  83.5 0.6 fusion.33
  84.1 2.8 %fusion.31 = (f32[3,384,1022]{1,2,0:T(8,128)S(1)}, f32[3,384,1022]{1,2,0:T(8,128)}) fusion(f32[3,384,1024]{1,2,0:T(8,128)S(1)} %bitcast.58), kind=kLoop, calls=%fused_computation.59 | loop fusion | bytes 18837504 | tf_op jit(solution)/shard_map/jit(_roll_static)/slice | solution.py:55
  86.9 6.7 %fusion.1 = f32[3,384,1024]{1,2,0:T(8,128)S(1)} fusion(f32[3,384,1]{1,2,0:T(1,128)S(1)} %get-tuple-element.9, f32[3,384,1023]{1,2,0:T(8,128)S(1)} %get-tuple-element.11, f32[3,384,1023]{1,2,0:T(8,128)S(1)} %get-tuple-element.10, f32[3,384,1]{1,2,0:T(1,128)S(1)} %get-tuple-element.8, f32[3,384,2]{1,2,0:T(2,128)S(1)} %get-tuple-element.5, ...), kind=kLoop, calls=%fused_computation.3 | loop fusion | flops 10616832 | bytes 23592960 | tf_op jit(solution)/shard_map/add | solution.py:54
  93.7 4.7 %fusion.10 = f32[3,384,8,128]{1,3,2,0:T(8,128)S(1)} fusion(f32[3,384,8,128]{1,3,2,0:T(8,128)S(1)} %bitcast.63, f32[128,128]{0,1:T(8,128)S(1)} %fusion.3), kind=kOutput, calls=%fused_computation.23 | convolution fusion | flops 1811939328 | bytes 9502720 | tf_op jit(solution)/shard_map/dot_general | solution.py:29
  98.4 0.1 fusion.29
  98.6 1.0 multiply_subtract_fusion
  99.6 3.2 %copy.34 = f32[3,384,1024]{1,0,2:T(4,128)S(1)} copy(f32[3,384,1024]{1,2,0:T(8,128)S(1)} %bitcast.64) | data formatting | bytes 9437184 | tf_op jit(solution)/shard_map/reshape | solution.py:64
  102.9 74.9 %all_to_all.23 = f32[3,384,1024]{1,0,2:T(4,128)} all-to-all(f32[3,384,1024]{1,0,2:T(4,128)S(1)} %copy.34), channel_id=1, replica_groups=mesh['blk'=8,'lines'=4] {'blk'}, dimensions={2} | all-to-all | bytes 9437184 | tf_op jit(solution)/shard_map/all_to_all | solution.py:65
  177.8 0.0 copy-start.1
  177.8 6.9 %copy.35 = f32[3,8,384,128]{3,2,1,0:T(8,128)} copy(f32[3,8,384,128]{2,0,3,1:T(4,128)} %bitcast.61) | data formatting | bytes 9437184 | tf_op jit(solution)/shard_map/all_to_all | solution.py:65
  184.7 0.0 copy-done.1
  184.7 0.0 copy-start
  184.7 4.9 %multiply_reduce_fusion = f32[128]{0:T(128)S(1)} fusion(f32[3,8,384,128]{2,0,3,1:T(4,128)} %bitcast.62, f32[128]{0:T(128)S(1)} %copy-done.1), kind=kLoop, calls=%fused_computation | loop fusion | flops 3538816 | bytes 4719616 | tf_op jit(solution)/shard_map/reduce_sum | solution.py:67
  189.6 0.0 copy-done
  189.6 2.5 %bitcast_multiply_fusion = f32[3,3072,128]{2,1,0:T(8,128)} fusion(f32[3,8,384,128]{3,2,1,0:T(8,128)S(1)} %copy-done, f32[128]{0:T(128)S(1)} %copy-done.1), kind=kLoop, calls=%fused_computation.6 | loop fusion | flops 1179648 | bytes 9437696 | tf_op jit(solution)/shard_map/mul | solution.py:66
  192.1 12.7 %psum.7 = f32[128]{0:T(128)S(1)} all-reduce(f32[128]{0:T(128)S(1)} %multiply_reduce_fusion), channel_id=1, replica_groups=mesh['blk'=8,'lines'=4] {'lines'}, use_global_device_ids=true, to_apply=%region_1.2 | all-reduce | flops 128 | bytes 1024 | tf_op jit(solution)/shard_map/psum | solution.py:68
  204.8 0.5 broadcast_multiply_fusion
  (12 shorter events, 0.1 us)
Async XLA Ops:
  20.8 60.0 %all-to-all-start = ((f32[8,3,384,128]{2,3,1,0:T(8,128)}), f32[8,3,384,128]{2,3,1,0:T(8,128)}, u32[]{:S(2)}, u32[]{:S(2)}) async-start(f32[8,3,384,128]{2,3,1,0:T(8,128)} %bitcast_dynamic-update-slice_fusion), calls=%async_computation | async-start | bytes 9437184 | tf_op jit(solution)/shard_map/all_to_all | solution.py:14
  177.8 6.9 %copy-start.1 = (f32[128]{0:T(128)S(1)}, f32[128]{0:T(128)}, u32[]{:S(2)}) copy-start(f32[128]{0:T(128)} %param.3) | copy-start | bytes 1540
  184.7 5.0 %copy-start = (f32[3,8,384,128]{3,2,1,0:T(8,128)S(1)}, f32[3,8,384,128]{3,2,1,0:T(8,128)}, u32[]{:S(2)}) copy-start(f32[3,8,384,128]{3,2,1,0:T(8,128)} %copy.35) | copy-start | bytes 14155780
